TPU v7x, 256 devices: a whole 4x4x8 slice. The times are simulated.
256 devices in a mesh: band: 64 (over z, y, core), tile: 4 (over x).
Axes of the slice: x: 4, y: 4, z: 8, core: 2. Of those that a mesh axis runs over, the one named last changes fastest.
Arguments:
- src_field: bfloat16 [4, 32, 1048576], P(None, None, ('band', 'tile')), may hold values from 0.0009994507 to 1
- weights: bfloat16 [65536, 128, 128], P(('band', 'tile')), may hold values from 0 to 0.05625
- block_slab: int32 [65536], P(('band', 'tile')), may hold values from 0 to 127
- block_dest: int32 [65536, 1], P(('band', 'tile')), may hold values from 0 to 255; in each aligned block of 256 rows (0 to 255, 256 to 511, ...) at most 2 rows name the same one
- block_tile: int32 [65536], P(('band', 'tile')), may hold values from 0 to 31
- prior_total: float32 [32, 1048576], P(None, ('band', 'tile')), may hold values from 0.2 to 4
- gamma_shape: float32 [1048576], P(('band', 'tile')), may hold values from 1 to 10
- gamma_scale: float32 [1048576], P(('band', 'tile')), may hold values from 0.05 to 0.6
Outputs:
- season_total: float32 [32, 1048576], P(None, ('band', 'tile'))
- spi_index: float32 [32, 1048576], P(None, ('band', 'tile'))
Inputs may be any that keep to these rules, and one draw needn't show every extreme that they name: `block_dest`: among the 256 blocks of any one device, each destination is named by at most 2 blocks, a bound that some block reaches.
All inputs are finite; a program needn't handle non-finite values.
Results may differ from a plain program's by a relative error of at most 0.00085.
Values may be sent and summed in bfloat16 or wider, within the bound.
A program may use at most 128 MiB of HBM per device.

v0:
```python
import jax
import jax.numpy as jnp
from jax import lax
from jax.sharding import PartitionSpec as P

PROB_FLOOR = 0.001
CENTRAL_NUMER = (
    -39.69683028665376,
    220.9460984245205,
    -275.9285104469687,
    138.357751867269,
    -30.66479806614716,
    2.506628277459239,
)
CENTRAL_DENOM = (
    -54.47609879822406,
    161.5858368580409,
    -155.6989798598866,
    66.80131188771972,
    -13.28068155288572,
    1.0,
)
TAIL_NUMER = (
    -0.007784894002430293,
    -0.3223964580411365,
    -2.400758277161838,
    -2.549671010429402,
    4.374664141464968,
    2.938163982698783,
)
TAIL_DENOM = (0.007784695709041462, 0.3224671290700398, 2.445134137142996, 3.754408661907416, 1.0)


def horner(coeffs, value):
    total = jnp.zeros_like(value) + coeffs[0]
    for coeff in coeffs[1:]:
        total = total * value + coeff
    return total


def normal_quantile(prob):
    centred = prob - 0.5
    square = centred * centred
    middle = centred * horner(CENTRAL_NUMER, square) / horner(CENTRAL_DENOM, square)
    lower_root = jnp.sqrt(-2.0 * jnp.log(prob))
    lower = horner(TAIL_NUMER, lower_root) / horner(TAIL_DENOM, lower_root)
    upper_root = jnp.sqrt(-2.0 * jnp.log(1.0 - prob))
    upper = -horner(TAIL_NUMER, upper_root) / horner(TAIL_DENOM, upper_root)
    result = jnp.where(prob < 0.02425, lower, middle)
    return jnp.where(prob > 0.97575, upper, result)


def lower_gamma(shape, value):
    border = shape + 1.0
    small_x = jnp.minimum(value, border)
    large_x = jnp.maximum(value, border)

    def series_step(index, carry):
        term, total = carry
        term = term * small_x / (shape + index)
        return (term, total + term)

    first = 1.0 / shape
    _, series = lax.fori_loop(1, 65, series_step, (first, first))
    series_value = series * jnp.exp(-small_x + shape * jnp.log(small_x) - lax.lgamma(shape))
    start_b = large_x + 1.0 - shape
    start_c = jnp.zeros_like(large_x) + 1e30
    start_d = 1.0 / start_b

    def fraction_step(index, carry):
        denom_b, lentz_c, lentz_d, accum = carry
        step_a = -index * (index - shape)
        denom_b = denom_b + 2.0
        lentz_d = 1.0 / (step_a * lentz_d + denom_b)
        lentz_c = denom_b + step_a / lentz_c
        return (denom_b, lentz_c, lentz_d, accum * lentz_d * lentz_c)

    _, _, _, fraction = lax.fori_loop(1, 65, fraction_step, (start_b, start_c, start_d, start_d))
    upper_value = fraction * jnp.exp(-large_x + shape * jnp.log(large_x) - lax.lgamma(shape))
    return jnp.where(value < border, series_value, 1.0 - upper_value)


def rank_within(owner_ids, groups):
    onehot = (owner_ids[:, None] == jnp.arange(groups, dtype=jnp.int32)[None, :]).astype(jnp.int32)
    before = jnp.cumsum(onehot, axis=0) - onehot
    return jnp.sum(before * onehot, axis=1)


def shards(
    src_field, weights, block_slab, block_dest, block_tile, prior_total, gamma_shape, gamma_scale
):
    band_count = lax.axis_size("band")
    tile_count = lax.axis_size("tile")
    devices = band_count * tile_count
    blocks = weights.shape[0]
    day_count, members, _ = src_field.shape
    own_tiles = gamma_shape.shape[0] // 128
    capacity = max(2, 2 * blocks // devices)
    gathered = lax.all_gather(src_field, "tile", axis=2, tiled=True)
    gathered = gathered.reshape(day_count, members, -1, 128)
    chosen = jnp.take(gathered, block_slab, axis=2)
    pieces = jnp.einsum("dmbs,bst->bmt", chosen, weights, preferred_element_type=jnp.float32)
    owner_ids = block_dest[:, 0]
    slot_rank = rank_within(owner_ids, devices)
    position = owner_ids * capacity + slot_rank
    outgoing = jnp.zeros((devices * capacity, members, 128), jnp.float32).at[position].set(pieces)
    labels = (
        jnp.zeros((devices * capacity,), jnp.float32)
        .at[position]
        .set(block_tile.astype(jnp.float32))
    )
    packed = outgoing.reshape(band_count, tile_count * capacity, members, 128)
    tile_tags = labels.reshape(band_count, tile_count * capacity)
    arrived, arrived_tags = (
        lax.all_to_all(
            packed.astype(jnp.bfloat16), "band", split_axis=0, concat_axis=0, tiled=True
        ).astype(packed.dtype),
        lax.all_to_all(
            tile_tags.astype(jnp.bfloat16), "band", split_axis=0, concat_axis=0, tiled=True
        ).astype(tile_tags.dtype),
    )
    column = jnp.arange(tile_count * capacity, dtype=jnp.int32) // capacity
    target = column[None, :] * own_tiles + arrived_tags.astype(jnp.int32)
    band_partial = jax.ops.segment_sum(
        arrived.reshape(-1, members, 128), target.reshape(-1), num_segments=tile_count * own_tiles
    )
    summed = lax.psum_scatter(band_partial, "tile", scatter_dimension=0, tiled=True)
    remapped = jnp.transpose(summed, (1, 0, 2)).reshape(members, own_tiles * 128)
    season_total = prior_total + remapped
    shape_full = jnp.broadcast_to(gamma_shape[None, :], season_total.shape)
    probability = lower_gamma(shape_full, season_total / gamma_scale[None, :])
    probability = jnp.clip(probability, PROB_FLOOR, 1.0 - PROB_FLOOR)
    spi_index = normal_quantile(probability)
    return (season_total, spi_index)


def solution(mesh):
    placed = (
        P(None, None, ("band", "tile")),
        P(("band", "tile"), None, None),
        P(("band", "tile")),
        P(("band", "tile"), None),
        P(("band", "tile")),
        P(None, ("band", "tile")),
        P(("band", "tile")),
        P(("band", "tile")),
    )
    return jax.shard_map(
        shards,
        mesh=mesh,
        in_specs=placed,
        out_specs=(P(None, ("band", "tile")), P(None, ("band", "tile"))),
        check_vma=False,
    )
```

profile of v0, /device:TPU:1, one launch (start us, length us, event | category | flops | bytes accessed | tf_op | source)
XLA Modules:
  0.0 382.7 jit_solution(5081914653799887709)
XLA Ops:
  7.2 0.7 all-gather.2.cloned.1.call-update
  7.9 0.8 copy.17
  9.0 0.7 convert_element_type.80
  9.7 0.9 fusion.38
  10.6 0.7 compare_select_fusion
  11.3 1.4 scatter_custom_fusion
  12.7 0.7 convert_element_type.93
  13.4 13.1 %all-to-all-start = ((bf16[64,1,8]{2,1,0:T(2,128)(2,1)}), bf16[64,1,8]{2,1,0:T(2,128)(2,1)S(1)}, u32[]{:S(2)}, u32[]{:S(2)}) async-start(bf16[64,1,8]{2,1,0:T(2,128)(2,1)} %convert_element_type.93), calls=%async_computation | async-start | bytes 65536 | tf_op jit(solution)/shard_map/all_to_all | solution.py:118
  26.5 0.7 compare_select_fusion.1
  27.2 0.7 compare_and_fusion
  27.9 36.3 %all-gather.2.cloned.1.call-done = bf16[4,32,16384]{2,1,0:T(8,128)(2,1)} async-done(((bf16[4,32,4096]{2,1,0:T(8,128)(2,1)}), bf16[4,32,16384]{2,1,0:T(8,128)(2,1)}) %all-gather.2.cloned.1.call-update) | async-done | bytes 4194320 | tf_op jit(solution)/shard_map/all_gather | solution.py:99
  64.2 4.9 %copy_bitcast_fusion = bf16[4,32,128,128]{3,1,2,0:T(8,128)(2,1)} fusion(bf16[4,32,16384]{2,1,0:T(8,128)(2,1)} %all-gather.2.cloned.1.call-done), kind=kLoop, calls=%fused_computation.15 | loop fusion | bytes 8388608 | tf_op jit(solution)/shard_map/reshape | solution.py:100
  69.1 10.8 %gather_fusion = bf16[256,4,32,128]{3,2,1,0:T(8,128)(2,1)} fusion(bf16[4,32,128,128]{3,1,2,0:T(8,128)(2,1)} %copy_bitcast_fusion, s32[1024]{0:T(1024)S(1)} %pad_clamp_fusion), kind=kCustom, calls=%fused_computation | custom fusion | bytes 16778240 | tf_op jit(solution)/shard_map/jit(_take)/gather | solution.py:101
  79.9 5.2 %convert_reduce_fusion = bf16[256,32,128]{2,1,0:T(8,128)(2,1)S(1)} fusion(bf16[256,4,32,128]{3,2,1,0:T(8,128)(2,1)} %gather_fusion, pred[256]{0:T(512)(128)(4,1)S(1)} %compare_and_fusion), kind=kLoop, calls=%fused_computation.14 | loop fusion | flops 11534336 | bytes 10486016 | tf_op jit(solution)/shard_map/dmbs,bst->bmt/reduce_sum | solution.py:102
  85.1 7.7 %fusion.5 = f32[256,32,128]{2,1,0:T(8,128)} fusion(bf16[256,128,128]{2,1,0:T(8,128)(2,1)} %param.13, bf16[256,32,128]{2,1,0:T(8,128)(2,1)S(1)} %convert_reduce_fusion), kind=kOutput, calls=%fused_computation.17 | convolution fusion | flops 268435456 | bytes 14680064 | tf_op jit(solution)/shard_map/dmbs,bst->bmt/dot_general | solution.py:102
  92.8 4.3 %broadcast_in_dim.52 = f32[512,32,128]{2,1,0:T(8,128)} broadcast(f32[]{:T(128)} %constant.75.clone.1), dimensions={} | broadcast | bytes 8388612 | tf_op jit(solution)/shard_map/broadcast_in_dim | solution.py:106
  97.1 33.5 %scatter_fusion = f32[512,32,128]{2,1,0:T(8,128)} fusion(f32[512,32,128]{2,1,0:T(8,128)} %broadcast_in_dim.52, s32[256]{0:T(256)S(1)} %bitcast.46, f32[256,32,128]{2,1,0:T(8,128)} %fusion.5), kind=kCustom, calls=%fused_computation.2 | custom fusion | bytes 12583936 | tf_op jit(solution)/shard_map/scatter | solution.py:106
  130.6 6.4 %convert_element_type.87 = bf16[512,32,128]{2,1,0:T(8,128)(2,1)} convert(f32[512,32,128]{2,1,0:T(8,128)} %scatter_fusion) | non-fusion elementwise | flops 2097152 | bytes 12582912 | tf_op jit(solution)/shard_map/convert_element_type | solution.py:116
  137.0 11.2 %all-to-all-start.1 = ((bf16[64,8,32,128]{3,2,1,0:T(8,128)(2,1)}), bf16[64,8,32,128]{3,2,1,0:T(8,128)(2,1)}, u32[]{:S(2)}, u32[]{:S(2)}) async-start(bf16[64,8,32,128]{3,2,1,0:T(8,128)(2,1)} %bitcast.38), calls=%async_computation.1 | async-start | bytes 8388608 | tf_op jit(solution)/shard_map/all_to_all | solution.py:115
  148.5 94.3 %all-to-all-done.1 = bf16[64,8,32,128]{3,2,1,0:T(8,128)(2,1)} async-done(((bf16[64,8,32,128]{3,2,1,0:T(8,128)(2,1)}), bf16[64,8,32,128]{3,2,1,0:T(8,128)(2,1)}, u32[]{:S(2)}, u32[]{:S(2)}) %all-to-all-start.1) | async-done | bytes 4194336 | tf_op jit(solution)/shard_map/all_to_all | solution.py:115
  242.9 6.6 %bitcast_convert_fusion = f32[512,32,128]{2,1,0:T(8,128)} fusion(bf16[64,8,32,128]{3,2,1,0:T(8,128)(2,1)} %all-to-all-done.1), kind=kLoop, calls=%fused_computation.16 | loop fusion | flops 2097152 | bytes 12582912 | tf_op jit(solution)/shard_map/reshape | solution.py:125
  249.8 44.8 %scatter_fusion.1 = f32[128,32,128]{2,1,0:T(8,128)S(1)} fusion(f32[128,32,128]{2,1,0:T(8,128)S(1)} %broadcast_in_dim.50, s32[512]{0:T(512)S(1)} %bitcast.44, f32[512,32,128]{2,1,0:T(8,128)} %bitcast_convert_fusion), kind=kCustom, calls=%fused_computation.3 | custom fusion | flops 2097152 | bytes 25167872 | tf_op jit(solution)/shard_map/scatter-add | solution.py:124
  294.6 1.3 copy-done
  296.0 28.8 %reduce-scatter.2.cloned.1.call-done = f32[32,32,128]{2,1,0:T(8,128)} async-done(((f32[128,32,128]{2,1,0:T(8,128)}), f32[32,32,128]{2,1,0:T(8,128)}) %reduce-scatter.2.cloned.1.call-update) | async-done | bytes 524304 | tf_op jit(solution)/shard_map/reduce_scatter | solution.py:127
  324.8 1.3 broadcast_minimum_fusion
  326.3 32.6 %while.37 = (s32[]{:T(128)}, f32[32,4096]{1,0:T(8,128)S(1)}, f32[32,4096]{1,0:T(8,128)S(1)}, f32[32,4096]{1,0:T(8,128)S(1)}, f32[32,4096]{1,0:T(8,128)S(1)}, /*index=5*/f32[4096]{0:T(1024)S(1)}, s32[]{:T(128)}, s32[]{:T(128)}) while((s32[]{:T(128)}, f32[32,4096]{1,0:T(8,128)S(1)}, f32[32,4096]{1,0:T(8,128)S(1)}, ...), condition=%wide.region_11.12_spmd.clone, body=%wide.region_10.11_spmd.clone.sunk | while | flops 1187846 | bytes 4243591 | solution.py:78
  326.3 0.5 multiply_multiply_fusion.6
  326.9 0.5 multiply_multiply_fusion.6
  328.4 0.5 multiply_multiply_fusion.6
  329.9 0.5 multiply_multiply_fusion.6
  359.0 13.3 %while.36 = (s32[]{:T(128)}, f32[32,4096]{1,0:T(8,128)S(1)}, f32[32,4096]{1,0:T(8,128)S(1)}, f32[32,4096]{1,0:T(8,128)S(1)}, f32[4096]{0:T(1024)S(1)}, /*index=5*/s32[]{:T(128)}) while((s32[]{:T(128)}, f32[32,4096]{1,0:T(8,128)S(1)}, f32[32,4096]{1,0:T(8,128)S(1)}, f32[32,4096]{1,0:T(8,128)S(1)}, f32[4096]{0:T(1024)S(1)}, ...), condition=%wide.region_9.10_spmd.clone, body=%wide.region_8.9_spmd.clone.sunk | while | flops 397315 | bytes 2670673 | solution.py:64
  372.3 3.6 select_select_fusion
  (286 shorter events, 40.9 us)
Async XLA Ops:
  7.2 57.0 %all-gather.2.cloned.1.call-start = ((), (), s32[]{:S(2)}) async-start(), calls=%async_computation.3 | async-start | bytes 5242880 | tf_op jit(solution)/shard_map/all_gather | solution.py:99
  13.4 123.6 %all-to-all-start = ((bf16[64,1,8]{2,1,0:T(2,128)(2,1)}), bf16[64,1,8]{2,1,0:T(2,128)(2,1)S(1)}, u32[]{:S(2)}, u32[]{:S(2)}) async-start(bf16[64,1,8]{2,1,0:T(2,128)(2,1)} %convert_element_type.93), calls=%async_computation | async-start | bytes 65536 | tf_op jit(solution)/shard_map/all_to_all | solution.py:118
  137.0 105.9 %all-to-all-start.1 = ((bf16[64,8,32,128]{3,2,1,0:T(8,128)(2,1)}), bf16[64,8,32,128]{3,2,1,0:T(8,128)(2,1)}, u32[]{:S(2)}, u32[]{:S(2)}) async-start(bf16[64,8,32,128]{3,2,1,0:T(8,128)(2,1)} %bitcast.38), calls=%async_computation.1 | async-start | bytes 8388608 | tf_op jit(solution)/shard_map/all_to_all | solution.py:115
  148.1 176.7 %reduce-scatter.2.cloned.1.call-start = ((), (), s32[]{:S(2)}) async-start(), calls=%async_computation.4 | async-start | bytes 2621440 | tf_op jit(solution)/shard_map/reduce_scatter | solution.py:127
  249.7 46.3 %copy-start.1 = (f32[4096]{0:T(1024)S(1)}, f32[4096]{0:T(1024)}, u32[]{:S(2)}) copy-start(f32[4096]{0:T(1024)} %param.18) | copy-start | bytes 49156
  249.7 75.1 %copy-start.3 = (f32[4096]{0:T(1024)S(1)}, f32[4096]{0:T(1024)}, u32[]{:S(2)}) copy-start(f32[4096]{0:T(1024)} %param.19) | copy-start | bytes 49156
  294.6 1.4 copy-start
  326.1 46.2 %copy-start.2 = (f32[32,4096]{1,0:T(8,128)}, f32[32,4096]{1,0:T(8,128)S(1)}, u32[]{:S(2)}) copy-start(f32[32,4096]{1,0:T(8,128)S(1)} %get-tuple-element.273) | copy-start | bytes 1572868
Sparse Core Ops, SparseCore 0:
  9.8 54.3 all-gather.1
  296.1 28.6 reduce-scatter.1
where the time goes:
time: 385 us; the launch traced here: 383 us
  waiting for transfers between devices  160 us (42%)
  other arithmetic  114 us (30%)
  local copies, waits for them, and re-layouts  58.4 us (15%)
  starting transfers between devices  24.4 us (6%)
  between operations  14.3 us (4%)
  matrix products  7.66 us (2%)
  loops' own time  4.34 us (1%)
    all_to_all x1, waiting for transfers between devices, shards(): lax.all_to_all(packed.astype(jnp.bfloat16), 'band', split_axis=0, concat_...  94.3 us
    scatter-add x1, other arithmetic, shards(): jax.ops.segment_sum(arrived.reshape(-1, members, 128), target.reshape(-1)...  44.8 us
    all_gather x1, waiting for transfers between devices, shards(): gathered = lax.all_gather(src_field, 'tile', axis=2, tiled=True)  36.3 us
    scatter x1, local copies, waits for them, and re-layouts, shards(): jnp.zeros((devices * capacity, members, 128), jnp.float32).at[position]  33.5 us
    mul x64, other arithmetic, fraction_step(): return (denom_b, lentz_c, lentz_d, accum * lentz_d * lentz_c)  29.9 us
    reduce_scatter x1, waiting for transfers between devices, shards(): lax.psum_scatter(band_partial, 'tile', scatter_dimension=0, tiled=True)  28.8 us
    all_to_all x1, starting transfers between devices, shards(): lax.all_to_all(tile_tags.astype(jnp.bfloat16), 'band', split_axis=0, conc...  13.1 us
    all_to_all x1, starting transfers between devices, shards(): lax.all_to_all(packed.astype(jnp.bfloat16), 'band', split_axis=0, concat_...  11.2 us
  transfers between devices with their start and end apart: 4, of which 3 were waited for; matrix products, arithmetic and copies ran while one was open for 21% of the time, Pallas kernels for 0%

commit v1 on v0

--- a/solution.py
+++ b/solution.py
@@ -29,6 +29,13 @@
     2.938163982698783,
 )
 TAIL_DENOM = (0.007784695709041462, 0.3224671290700398, 2.445134137142996, 3.754408661907416, 1.0)
+
+
+def patches_pass(tile_in):
+    lanes = []
+    for _ in range(jax.lax.axis_size("tile")):
+        lanes.append(tile_in)
+    return jnp.concatenate(jax.lax.all_to_all(jnp.stack(lanes), "tile", 0, 0), axis=2)
 
 
 def horner(coeffs, value):
@@ -96,7 +103,7 @@
     day_count, members, _ = src_field.shape
     own_tiles = gamma_shape.shape[0] // 128
     capacity = max(2, 2 * blocks // devices)
-    gathered = lax.all_gather(src_field, "tile", axis=2, tiled=True)
+    gathered = patches_pass(src_field)
     gathered = gathered.reshape(day_count, members, -1, 128)
     chosen = jnp.take(gathered, block_slab, axis=2)
     pieces = jnp.einsum("dmbs,bst->bmt", chosen, weights, preferred_element_type=jnp.float32)

time: 385 us -> 415 us (1.078)
  local copies, waits for them, and re-layouts: 58.4 us -> 79.3 us
  starting transfers between devices: 24.4 us -> 30.8 us
  waiting for transfers between devices: 160 us -> 166 us
    all_to_all x0 -> x1, waiting for transfers between devices: none -> 44.1 us  [patches_pass(): jax.lax.all_to_all(jnp.stack(lanes), 'tile', 0, 0)]
    all_gather x1 -> x0, waiting for transfers between devices: 36.3 us -> none  [shards(): gathered = lax.all_gather(src_field, 'tile', axis=2, tiled=True)]
    another operation x3 -> x6, local copies, waits for them, and re-layouts: 0.03 us -> 19 us  [the longest x2 15.3 us: shards(): gathered = gathered.reshape(day_count, members, -1, 128)]
    all_to_all x0 -> x1, starting transfers between devices: none -> 4.99 us  [patches_pass(): jax.lax.all_to_all(jnp.stack(lanes), 'tile', 0, 0)]
  transfers between devices with their start and end apart: 4 -> 4, of which waited for: 3 -> 3; matrix products, arithmetic and copies ran while one was open for 21% -> 23% of each run, Pallas kernels for 0% -> 0%
where the time goes in v1:
time: 415 us; the launch traced here: 413 us
  waiting for transfers between devices  166 us (40%)
  other arithmetic  110 us (27%)
  local copies, waits for them, and re-layouts  79.3 us (19%)
  starting transfers between devices  30.8 us (7%)
  between operations  14.3 us (3%)
  matrix products  7.66 us (2%)
  loops' own time  4.34 us (1%)
    all_to_all x1, waiting for transfers between devices, shards(): lax.all_to_all(packed.astype(jnp.bfloat16), 'band', split_axis=0, concat_...  94.3 us
    scatter-add x1, other arithmetic, shards(): jax.ops.segment_sum(arrived.reshape(-1, members, 128), target.reshape(-1)...  44.8 us
    all_to_all x1, waiting for transfers between devices, patches_pass(): jax.lax.all_to_all(jnp.stack(lanes), 'tile', 0, 0)  44.1 us
    scatter x1, local copies, waits for them, and re-layouts, shards(): jnp.zeros((devices * capacity, members, 128), jnp.float32).at[position]  33.5 us
    mul x64, other arithmetic, fraction_step(): return (denom_b, lentz_c, lentz_d, accum * lentz_d * lentz_c)  29.9 us
    reduce_scatter x1, waiting for transfers between devices, shards(): lax.psum_scatter(band_partial, 'tile', scatter_dimension=0, tiled=True)  27.9 us
    all_to_all x1, starting transfers between devices, shards(): lax.all_to_all(tile_tags.astype(jnp.bfloat16), 'band', split_axis=0, conc...  15.4 us
    another operation x2, local copies, waits for them, and re-layouts, shards(): gathered = gathered.reshape(day_count, members, -1, 128)  15.3 us
  transfers between devices with their start and end apart: 4, of which 3 were waited for; matrix products, arithmetic and copies ran while one was open for 23% of the time, Pallas kernels for 0%

profile of v1, /device:TPU:1, one launch (start us, length us, event | category | flops | bytes accessed | tf_op | source)
XLA Modules:
  0.0 412.9 jit_solution(10610490001445541663)
XLA Ops:
  7.2 3.7 stack.2
  10.9 5.0 %all-to-all-start.1 = ((bf16[4,4,32,4096]{3,2,1,0:T(8,128)(2,1)}), bf16[4,4,32,4096]{3,2,1,0:T(8,128)(2,1)}, u32[]{:S(2)}, u32[]{:S(2)}) async-start(bf16[4,4,32,4096]{3,2,1,0:T(8,128)(2,1)} %stack.2), calls=%async_computation.1 | async-start | bytes 8388608 | tf_op jit(solution)/shard_map/all_to_all | solution.py:38
  16.5 1.4 scatter_custom_fusion
  18.0 0.7 convert_element_type.93
  18.7 44.1 %all-to-all-done.1 = bf16[4,4,32,4096]{3,2,1,0:T(8,128)(2,1)} async-done(((bf16[4,4,32,4096]{3,2,1,0:T(8,128)(2,1)}), bf16[4,4,32,4096]{3,2,1,0:T(8,128)(2,1)}, u32[]{:S(2)}, u32[]{:S(2)}) %all-to-all-start.1) | async-done | bytes 4194336 | tf_op jit(solution)/shard_map/all_to_all | solution.py:38
  62.8 15.4 %all-to-all-start = ((bf16[64,1,8]{2,1,0:T(2,128)(2,1)}), bf16[64,1,8]{2,1,0:T(2,128)(2,1)S(1)}, u32[]{:S(2)}, u32[]{:S(2)}) async-start(bf16[64,1,8]{2,1,0:T(2,128)(2,1)} %convert_element_type.93), calls=%async_computation | async-start | bytes 65536 | tf_op jit(solution)/shard_map/all_to_all | solution.py:125
  78.2 7.4 %copy.21 = bf16[4,32,4,4096]{3,2,1,0:T(4,128)(2,1)} copy(bf16[4,32,4,4096]{3,1,0,2:T(8,128)(2,1)} %bitcast.8) | data formatting | bytes 8388608 | tf_op jit(solution)/shard_map/reshape | solution.py:38
  85.6 8.4 %reshape_reshape.3 = bf16[4,32,128,128]{3,2,1,0:T(8,128)(2,1)} reshape(bf16[4,32,4,4096]{3,2,1,0:T(4,128)(2,1)} %copy.21) | data formatting | bytes 8388608 | tf_op jit(solution)/shard_map/reshape;reshape | solution.py:107
  94.0 6.9 %copy.22 = bf16[4,32,128,128]{3,1,2,0:T(8,128)(2,1)} copy(bf16[4,32,128,128]{3,2,1,0:T(8,128)(2,1)} %reshape_reshape.3) | data formatting | bytes 8388608 | tf_op jit(solution)/shard_map/reshape;reshape | solution.py:107
  100.9 10.8 %gather_fusion = bf16[256,4,32,128]{3,2,1,0:T(8,128)(2,1)} fusion(bf16[4,32,128,128]{3,1,2,0:T(8,128)(2,1)} %copy.22, s32[1024]{0:T(1024)S(1)} %pad_clamp_fusion), kind=kCustom, calls=%fused_computation | custom fusion | bytes 16778240 | tf_op jit(solution)/shard_map/jit(_take)/gather | solution.py:108
  111.7 5.2 %convert_reduce_fusion = bf16[256,32,128]{2,1,0:T(8,128)(2,1)S(1)} fusion(bf16[256,4,32,128]{3,2,1,0:T(8,128)(2,1)} %gather_fusion, pred[256]{0:T(512)(128)(4,1)S(1)} %compare_and_fusion), kind=kLoop, calls=%fused_computation.14 | loop fusion | flops 11534336 | bytes 10486016 | tf_op jit(solution)/shard_map/dmbs,bst->bmt/reduce_sum | solution.py:109
  116.9 7.7 %fusion.5 = f32[256,32,128]{2,1,0:T(8,128)} fusion(bf16[256,128,128]{2,1,0:T(8,128)(2,1)} %param.13, bf16[256,32,128]{2,1,0:T(8,128)(2,1)S(1)} %convert_reduce_fusion), kind=kOutput, calls=%fused_computation.16 | convolution fusion | flops 268435456 | bytes 14680064 | tf_op jit(solution)/shard_map/dmbs,bst->bmt/dot_general | solution.py:109
  124.6 4.3 %broadcast_in_dim.52 = f32[512,32,128]{2,1,0:T(8,128)} broadcast(f32[]{:T(128)} %constant.75.clone.1), dimensions={} | broadcast | bytes 8388612 | tf_op jit(solution)/shard_map/broadcast_in_dim | solution.py:113
  128.9 33.5 %scatter_fusion = f32[512,32,128]{2,1,0:T(8,128)} fusion(f32[512,32,128]{2,1,0:T(8,128)} %broadcast_in_dim.52, s32[256]{0:T(256)S(1)} %bitcast.42, f32[256,32,128]{2,1,0:T(8,128)} %fusion.5), kind=kCustom, calls=%fused_computation.2 | custom fusion | bytes 12583936 | tf_op jit(solution)/shard_map/scatter | solution.py:113
  162.4 6.4 %convert_element_type.87 = bf16[512,32,128]{2,1,0:T(8,128)(2,1)} convert(f32[512,32,128]{2,1,0:T(8,128)} %scatter_fusion) | non-fusion elementwise | flops 2097152 | bytes 12582912 | tf_op jit(solution)/shard_map/convert_element_type | solution.py:123
  168.8 10.4 %all-to-all-start.2 = ((bf16[64,8,32,128]{3,2,1,0:T(8,128)(2,1)}), bf16[64,8,32,128]{3,2,1,0:T(8,128)(2,1)}, u32[]{:S(2)}, u32[]{:S(2)}) async-start(bf16[64,8,32,128]{3,2,1,0:T(8,128)(2,1)} %bitcast.34), calls=%async_computation.2 | async-start | bytes 8388608 | tf_op jit(solution)/shard_map/all_to_all | solution.py:122
  179.6 94.3 %all-to-all-done.2 = bf16[64,8,32,128]{3,2,1,0:T(8,128)(2,1)} async-done(((bf16[64,8,32,128]{3,2,1,0:T(8,128)(2,1)}), bf16[64,8,32,128]{3,2,1,0:T(8,128)(2,1)}, u32[]{:S(2)}, u32[]{:S(2)}) %all-to-all-start.2) | async-done | bytes 4194336 | tf_op jit(solution)/shard_map/all_to_all | solution.py:122
  273.9 6.6 %bitcast_convert_fusion = f32[512,32,128]{2,1,0:T(8,128)} fusion(bf16[64,8,32,128]{3,2,1,0:T(8,128)(2,1)} %all-to-all-done.2), kind=kLoop, calls=%fused_computation.15 | loop fusion | flops 2097152 | bytes 12582912 | tf_op jit(solution)/shard_map/reshape | solution.py:132
  280.8 44.8 %scatter_fusion.1 = f32[128,32,128]{2,1,0:T(8,128)S(1)} fusion(f32[128,32,128]{2,1,0:T(8,128)S(1)} %broadcast_in_dim.50, s32[512]{0:T(512)S(1)} %bitcast.40, f32[512,32,128]{2,1,0:T(8,128)} %bitcast_convert_fusion), kind=kCustom, calls=%fused_computation.3 | custom fusion | flops 2097152 | bytes 25167872 | tf_op jit(solution)/shard_map/scatter-add | solution.py:131
  325.7 1.3 copy-done
  327.1 27.9 %reduce-scatter.2.cloned.1.call-done = f32[32,32,128]{2,1,0:T(8,128)} async-done(((f32[128,32,128]{2,1,0:T(8,128)}), f32[32,32,128]{2,1,0:T(8,128)}) %reduce-scatter.2.cloned.1.call-update) | async-done | bytes 524304 | tf_op jit(solution)/shard_map/reduce_scatter | solution.py:134
  355.0 1.3 broadcast_minimum_fusion
  356.5 32.6 %while.37 = (s32[]{:T(128)}, f32[32,4096]{1,0:T(8,128)S(1)}, f32[32,4096]{1,0:T(8,128)S(1)}, f32[32,4096]{1,0:T(8,128)S(1)}, f32[32,4096]{1,0:T(8,128)S(1)}, /*index=5*/f32[4096]{0:T(1024)S(1)}, s32[]{:T(128)}, s32[]{:T(128)}) while((s32[]{:T(128)}, f32[32,4096]{1,0:T(8,128)S(1)}, f32[32,4096]{1,0:T(8,128)S(1)}, ...), condition=%wide.region_11.12_spmd.clone, body=%wide.region_10.11_spmd.clone.sunk | while | flops 1187846 | bytes 4243591 | solution.py:85
  356.5 0.5 multiply_multiply_fusion.6
  358.1 0.5 multiply_multiply_fusion.6
  359.6 0.5 multiply_multiply_fusion.6
  361.1 0.5 multiply_multiply_fusion.6
  362.7 0.5 multiply_multiply_fusion.6
  364.2 0.5 multiply_multiply_fusion.6
  364.7 0.5 multiply_multiply_fusion.6
  389.2 13.3 %while.36 = (s32[]{:T(128)}, f32[32,4096]{1,0:T(8,128)S(1)}, f32[32,4096]{1,0:T(8,128)S(1)}, f32[32,4096]{1,0:T(8,128)S(1)}, f32[4096]{0:T(1024)S(1)}, /*index=5*/s32[]{:T(128)}) while((s32[]{:T(128)}, f32[32,4096]{1,0:T(8,128)S(1)}, f32[32,4096]{1,0:T(8,128)S(1)}, f32[32,4096]{1,0:T(8,128)S(1)}, f32[4096]{0:T(1024)S(1)}, ...), condition=%wide.region_9.10_spmd.clone, body=%wide.region_8.9_spmd.clone.sunk | while | flops 397315 | bytes 2670673 | solution.py:71
  402.5 3.6 select_select_fusion
  (294 shorter events, 39.8 us)
Async XLA Ops:
  10.9 5.0 %copy-start.4 = (s32[256,1]{0,1:T(1,128)S(1)}, s32[256,1]{0,1:T(1,128)}, u32[]{:S(2)}) copy-start(s32[256,1]{0,1:T(1,128)} %param.15) | copy-start | bytes 3076
  10.9 5.4 %copy-start.5 = (s32[256]{0:T(256)S(1)}, s32[256]{0:T(256)}, u32[]{:S(2)}) copy-start(s32[256]{0:T(256)} %param.16) | copy-start | bytes 3076
  10.9 7.8 %copy-start.6 = (s32[256]{0:T(256)S(1)}, s32[256]{0:T(256)}, u32[]{:S(2)}) copy-start(s32[256]{0:T(256)} %param.14) | copy-start | bytes 3076
  10.9 51.9 %all-to-all-start.1 = ((bf16[4,4,32,4096]{3,2,1,0:T(8,128)(2,1)}), bf16[4,4,32,4096]{3,2,1,0:T(8,128)(2,1)}, u32[]{:S(2)}, u32[]{:S(2)}) async-start(bf16[4,4,32,4096]{3,2,1,0:T(8,128)(2,1)} %stack.2), calls=%async_computation.1 | async-start | bytes 8388608 | tf_op jit(solution)/shard_map/all_to_all | solution.py:38
  62.8 106.0 %all-to-all-start = ((bf16[64,1,8]{2,1,0:T(2,128)(2,1)}), bf16[64,1,8]{2,1,0:T(2,128)(2,1)S(1)}, u32[]{:S(2)}, u32[]{:S(2)}) async-start(bf16[64,1,8]{2,1,0:T(2,128)(2,1)} %convert_element_type.93), calls=%async_computation | async-start | bytes 65536 | tf_op jit(solution)/shard_map/all_to_all | solution.py:125
  168.8 105.1 %all-to-all-start.2 = ((bf16[64,8,32,128]{3,2,1,0:T(8,128)(2,1)}), bf16[64,8,32,128]{3,2,1,0:T(8,128)(2,1)}, u32[]{:S(2)}, u32[]{:S(2)}) async-start(bf16[64,8,32,128]{3,2,1,0:T(8,128)(2,1)} %bitcast.34), calls=%async_computation.2 | async-start | bytes 8388608 | tf_op jit(solution)/shard_map/all_to_all | solution.py:122
  179.2 175.8 %reduce-scatter.2.cloned.1.call-start = ((), (), s32[]{:S(2)}) async-start(), calls=%async_computation.4 | async-start | bytes 2621440 | tf_op jit(solution)/shard_map/reduce_scatter | solution.py:134
  280.8 46.3 %copy-start.1 = (f32[4096]{0:T(1024)S(1)}, f32[4096]{0:T(1024)}, u32[]{:S(2)}) copy-start(f32[4096]{0:T(1024)} %param.18) | copy-start | bytes 49156
  280.8 74.2 %copy-start.3 = (f32[4096]{0:T(1024)S(1)}, f32[4096]{0:T(1024)}, u32[]{:S(2)}) copy-start(f32[4096]{0:T(1024)} %param.19) | copy-start | bytes 49156
  325.7 1.4 copy-start
  356.3 46.2 %copy-start.2 = (f32[32,4096]{1,0:T(8,128)}, f32[32,4096]{1,0:T(8,128)S(1)}, u32[]{:S(2)}) copy-start(f32[32,4096]{1,0:T(8,128)S(1)} %get-tuple-element.273) | copy-start | bytes 1572868
Sparse Core Ops, SparseCore 0:
  327.2 27.8 reduce-scatter.1
